TPU v7x, 512 devices: a whole 4x8x8 slice. The times are simulated.
512 devices in a mesh: group: 8 (over z), ray: 64 (over y, x, core).
Axes of the slice: x: 4, y: 8, z: 8, core: 2. Of those that a mesh axis runs over, the one named last changes fastest.
Arguments:
- bricks: bfloat16 [16384, 4096], P(('group', 'ray')), may hold values from -6 to 6
- work_bricks: int32 [8, 128], P('group', 'ray'), may hold values from 0 to 16383, as said below
- interp: bfloat16 [32768, 5, 512], P(('group', 'ray')), may hold values from 0 to 0.25
- tile_slot: int32 [32768, 5], P(('group', 'ray')), may hold values from 0 to 127, as said below
- spacing: float32 [32768, 40], P(('group', 'ray')), may hold values from 0.02 to 0.3
- targets: float32 [3, 32768], P(None, ('group', 'ray')), may hold values from 0 to 1
- weight_in: bfloat16 [64, 256], replicated, may hold values from -0.75 to 0.75
- weight_mid: bfloat16 [256, 256], replicated, may hold values from -0.375 to 0.375
- weight_out: bfloat16 [256, 4], replicated, may hold values from -0.375 to 0.375
Outputs:
- brick_grad: float32 [16384, 4096], P(('group', 'ray'))
Inputs may be any that keep to these rules, and one draw needn't show every extreme that they name: `work_bricks`: slot j of image group g is held by ray index j // 2 of the group, and its brick's owner, the device brick // 32 counted over group then ray, has that same ray index. Among the 2 slots of one device at most 2 name bricks owned in one image group, and on every device exactly 2 do for some group. `tile_slot`: of the 320 tiles of one device, at most 10 name slots held by one device of the group, and on every device some holder is named exactly 10 times.
All inputs are finite; a program needn't handle non-finite values.
Results may differ from a plain program's by a relative error of at most 0.0022.
Values may be sent and summed in bfloat16 or wider, within the bound.
A program may use at most 64 MiB of HBM per device.

v0:
```python
import jax
import jax.numpy as jnp
from jax import lax
from jax.sharding import PartitionSpec as P


def silu_slope(pre_act):
    logistic = jax.nn.sigmoid(pre_act)
    return logistic * (1.0 + pre_act * (1.0 - logistic))


def composite_loss(raw_out, spacing, targets):
    density = jax.nn.softplus(raw_out[:, :, 0])
    shading = jax.nn.sigmoid(raw_out[:, :, 1:4])
    optical = density * spacing
    before_sum = jnp.cumsum(optical, axis=1) - optical
    ray_weight = jnp.exp(-before_sum) * (1.0 - jnp.exp(-optical))
    colour = jnp.sum(ray_weight[:, :, None] * shading, axis=1)
    return 0.5 * jnp.sum((colour - targets.T) ** 2)


def feature_grad(features, spacing, targets, weight_in, weight_mid, weight_out):
    pre_first = jnp.dot(features, weight_in, preferred_element_type=jnp.float32)
    act_first = jax.nn.silu(pre_first).astype(jnp.bfloat16)
    pre_second = jnp.dot(act_first, weight_mid, preferred_element_type=jnp.float32)
    act_second = jax.nn.silu(pre_second).astype(jnp.bfloat16)
    raw_out = jnp.dot(act_second, weight_out, preferred_element_type=jnp.float32)
    ray_count = spacing.shape[0]
    raw_grad = jax.grad(composite_loss)(raw_out.reshape(ray_count, -1, 4), spacing, targets)
    raw_grad = raw_grad.reshape(-1, 4).astype(jnp.bfloat16)
    grad_second = jnp.dot(raw_grad, weight_out.T, preferred_element_type=jnp.float32)
    slope_second = (grad_second * silu_slope(pre_second)).astype(jnp.bfloat16)
    grad_first = jnp.dot(slope_second, weight_mid.T, preferred_element_type=jnp.float32)
    slope_first = (grad_first * silu_slope(pre_first)).astype(jnp.bfloat16)
    return jnp.dot(slope_first, weight_in.T, preferred_element_type=jnp.float32).astype(
        jnp.bfloat16
    )


def earlier_equal(labels):
    order_index = jnp.arange(labels.shape[0])
    matches = (labels[:, None] == labels[None, :]) & (order_index[None, :] < order_index[:, None])
    return jnp.sum(matches.astype(jnp.int32), axis=1)


def per_device(
    bricks, work_bricks, interp, tile_slot, spacing, targets, weight_in, weight_mid, weight_out
):
    own_count = bricks.shape[0]
    row_width = bricks.shape[1]
    held_count = work_bricks.shape[1]
    channels = weight_in.shape[0]
    voxels = row_width // channels
    rays_dev, segments, span = interp.shape
    samples = span // voxels
    tiles_dev = rays_dev * segments
    group_size = lax.axis_size("group")
    ray_size = lax.axis_size("ray")
    per_owner = 1 + (held_count + group_size - 2) // group_size
    entries = work_bricks[0]
    owner_group = entries // own_count // ray_size
    local_id = entries % own_count
    entry_rank = earlier_equal(owner_group)
    requests = (
        jnp.full((group_size, per_owner), -1, jnp.int32).at[owner_group, entry_rank].set(local_id)
    )
    asked = lax.all_to_all(requests, "group", split_axis=0, concat_axis=0, tiled=True)
    wanted = asked >= 0
    picked = jnp.take(bricks, jnp.where(wanted, asked, 0).reshape(-1), axis=0)
    picked = jnp.where(
        wanted[:, :, None],
        picked.reshape(group_size, per_owner, row_width),
        jnp.zeros((), jnp.bfloat16),
    )
    fetched = lax.all_to_all(picked, "group", split_axis=0, concat_axis=0, tiled=True)
    holdings = fetched[owner_group, entry_rank]
    group_set = lax.all_gather(holdings, "ray", axis=0, tiled=True)
    weights_tiles = interp.reshape(tiles_dev, samples, voxels)
    slots = tile_slot.reshape(-1)
    tiles = jnp.take(group_set, slots, axis=0).reshape(tiles_dev, voxels, channels)
    made = jnp.einsum("tiv,tvc->tic", weights_tiles, tiles, preferred_element_type=jnp.float32)
    features = made.astype(jnp.bfloat16).reshape(-1, channels)
    tile_gradients = feature_grad(features, spacing, targets, weight_in, weight_mid, weight_out)
    grads_tiles = tile_gradients.reshape(tiles_dev, samples, channels)
    outer = jnp.einsum(
        "tiv,tic->tvc", weights_tiles, grads_tiles, preferred_element_type=jnp.float32
    )
    group_grad = jax.ops.segment_sum(
        outer.reshape(tiles_dev, row_width), slots, num_segments=held_count * ray_size
    )
    slot_grad = lax.psum_scatter(group_grad, "ray", scatter_dimension=0, tiled=True)
    outgoing = (
        jnp.zeros((group_size, per_owner, row_width), jnp.float32)
        .at[owner_group, entry_rank]
        .set(slot_grad)
    )
    arrived = lax.all_to_all(outgoing, "group", split_axis=0, concat_axis=0, tiled=True).reshape(
        group_size * per_owner, row_width
    )
    destination = jnp.where(wanted, asked, own_count).reshape(-1)
    return jax.ops.segment_sum(arrived, destination, num_segments=own_count + 1)[:own_count]


def solution(mesh):
    in_specs = (
        P(("group", "ray"), None),
        P("group", "ray"),
        P(("group", "ray"), None, None),
        P(("group", "ray"), None),
        P(("group", "ray"), None),
        P(None, ("group", "ray")),
        P(),
        P(),
        P(),
    )
    out_specs = P(("group", "ray"), None)
    return jax.shard_map(
        per_device, mesh=mesh, in_specs=in_specs, out_specs=out_specs, check_vma=False
    )
```

profile of v0, /device:TPU:31, one launch (start us, length us, event | category | flops | bytes accessed | tf_op | source)
XLA Modules:
  0.0 438.0 jit_solution(10257369317479114690)
XLA Ops:
  9.6 16.4 %all_to_all.25 = s32[8,1,2]{2,1,0:T(1,128)S(1)} all-to-all(s32[8,1,2]{2,1,0:T(1,128)S(1)} %copy.55), channel_id=1, replica_groups=mesh['group'=8,'ray'=64] {'group'}, dimensions={0} | all-to-all | bytes 128 | tf_op jit(solution)/shard_map/all_to_all | solution.py:67
  29.0 10.4 %all_to_all.26 = bf16[8,2,4096]{2,1,0:T(2,128)(2,1)S(1)} all-to-all(bf16[8,2,4096]{2,1,0:T(2,128)(2,1)S(1)} %broadcast_select_fusion.2), channel_id=1, replica_groups=mesh['group'=8,'ray'=64] {'group'}, dimensions={0} | all-to-all | bytes 262144 | tf_op jit(solution)/shard_map/all_to_all | solution.py:75
  43.4 77.1 %all-gather.3.cloned.1.call-done = bf16[64,2,4096]{2,1,0:T(2,128)(2,1)} async-done(((bf16[1,2,4096]{2,1,0:T(2,128)(2,1)}), bf16[64,2,4096]{2,1,0:T(2,128)(2,1)}) %all-gather.3.cloned.1.call-update) | async-done | bytes 1048592 | tf_op jit(solution)/shard_map/all_gather | solution.py:77
  121.9 3.9 gather_fusion.2
  125.8 3.3 copy.61
  129.1 2.0 broadcast_select_fusion
  131.1 10.1 %copy.63 = bf16[320,64,64]{2,1,0:T(8,128)(2,1)} copy(bf16[320,64,64]{0,2,1:T(8,128)(2,1)} %broadcast_select_fusion) | data formatting | bytes 5242880 | tf_op jit(solution)/shard_map/jit(_take)/select_n | solution.py:80
  141.2 4.3 fusion.8
  145.5 1.7 fusion.4
  147.3 1.5 copy-done.8
  150.2 1.6 reshape.279
  153.2 1.6 reduce_window_sum.22
  156.6 1.6 fusion.12
  160.2 1.6 reduce_window_sum.23
  162.7 1.5 add_convert_fusion
  164.3 1.6 convert_element_type.36
  165.8 4.0 fusion
  169.8 3.3 convolution_convert_fusion
  174.4 4.9 %convolution_bitcast_fusion = f32[320,64,64]{1,2,0:T(8,128)} fusion(bf16[320,8,64]{2,1,0:T(8,128)(2,1)S(1)} %copy-done.1, bf16[2560,64]{1,0:T(8,128)(2,1)S(1)} %copy.66), kind=kOutput, calls=%fused_computation.11 | convolution fusion | flops 20971520 | bytes 5898240 | tf_op jit(solution)/shard_map/tiv,tic->tvc/dot_general | solution.py:85
  179.3 11.8 %copy.67 = f32[320,64,64]{0,2,1:T(8,128)} copy(f32[320,64,64]{1,2,0:T(8,128)} %convolution_bitcast_fusion) | data formatting | bytes 10485760 | tf_op jit(solution)/shard_map/tiv,tic->tvc/dot_general | solution.py:85
  191.1 6.2 %copy.68 = f32[320,4096]{1,0:T(8,128)} copy(f32[320,4096]{0,1:T(8,128)} %bitcast.97) | data formatting | bytes 10485760 | tf_op jit(solution)/shard_map/reshape | solution.py:89
  197.4 10.6 %scatter_custom_fusion.1 = f32[128,4096]{1,0:T(8,128)} fusion(s32[320]{0:T(512)S(1)} %reshape.313, f32[320,4096]{1,0:T(8,128)} %copy.68, f32[]{:T(128)} %constant.85.clone.1), kind=kCustom, calls=%fused_computation.23 | custom fusion | flops 1310720 | bytes 2097664 | tf_op jit(solution)/shard_map/scatter-add | solution.py:88
  209.9 198.0 %all-reduce.5.cloned.1.call-done = f32[128,4096]{1,0:T(8,128)} async-done(((f32[128,4096]{1,0:T(8,128)}), f32[128,4096]{1,0:T(8,128)}) %all-reduce.5.cloned.1.call-update) | async-done | bytes 2097168
  409.6 19.3 %all_to_all.27 = f32[8,2,4096]{2,1,0:T(2,128)S(1)} all-to-all(f32[8,2,4096]{2,1,0:T(2,128)S(1)} %scatter_fusion.1), channel_id=1, replica_groups=mesh['group'=8,'ray'=64] {'group'}, dimensions={0} | all-to-all | bytes 524288 | tf_op jit(solution)/shard_map/all_to_all | solution.py:97
  (67 shorter events, 25.5 us)
Async XLA Ops:
  6.5 21.2 %copy-start = (bf16[32,4096]{1,0:T(8,128)(2,1)S(1)}, bf16[32,4096]{1,0:T(8,128)(2,1)}, u32[]{:S(2)}) copy-start(bf16[32,4096]{1,0:T(8,128)(2,1)} %param.9) | copy-start | bytes 786436
  6.5 34.2 %copy-start.5 = (s32[64,5]{0,1:T(8,128)S(1)}, s32[64,5]{0,1:T(8,128)}, u32[]{:S(2)}) copy-start(s32[64,5]{0,1:T(8,128)} %param.12) | copy-start | bytes 3844
  6.5 34.6 %copy-start.2 = (bf16[64,5,512]{2,0,1:T(8,128)(2,1)S(1)}, bf16[64,5,512]{2,0,1:T(8,128)(2,1)}, u32[]{:S(2)}) copy-start(bf16[64,5,512]{2,0,1:T(8,128)(2,1)} %param.11) | copy-start | bytes 983044
  6.5 113.9 %all-gather.3.cloned.1.call-start = ((), (), s32[]{:S(2)}) async-start(), calls=%async_computation.3 | async-start | bytes 1064960 | tf_op jit(solution)/shard_map/all_gather | solution.py:77
  8.8 33.8 %copy-start.4 = (f32[64,40]{0,1:T(8,128)S(1)}, f32[64,40]{0,1:T(8,128)}, u32[]{:S(2)}) copy-start(f32[64,40]{0,1:T(8,128)} %param.13) | copy-start | bytes 30724
  40.7 367.2 %all-reduce.5.cloned.1.call-start = ((), (), s32[]{:S(2)}) async-start(), calls=%async_computation.4 | async-start | bytes 4194304
  131.1 10.1 %copy-start.1 = (bf16[320,8,64]{2,1,0:T(8,128)(2,1)S(1)}, bf16[320,8,64]{2,1,0:T(8,128)(2,1)}, u32[]{:S(2)}) copy-start(bf16[320,8,64]{2,1,0:T(8,128)(2,1)} %reshape.277) | copy-start | bytes 983044
  145.5 3.3 copy-start.7
  147.3 1.5 copy-start.8
  148.8 7.8 %copy-start.6 = (f32[3,64]{1,0:T(4,128)S(1)}, f32[3,64]{1,0:T(4,128)}, u32[]{:S(2)}) copy-start(f32[3,64]{1,0:T(4,128)} %param.14) | copy-start | bytes 2308
  158.2 0.6 copy-start.3
Sparse Core Ops, SparseCore 0:
  40.8 79.5 all-gather.2
  208.1 199.7 all-reduce.4
where the time goes:
time: 439 us; the launch traced here: 438 us
  waiting for transfers between devices  275 us (63%)
  local copies, waits for them, and re-layouts  53.5 us (12%)
  blocking collectives  46.1 us (11%)
  other arithmetic  29.4 us (7%)
  matrix products  19.6 us (4%)
  between operations  14.3 us (3%)
    unnamed x3, waiting for transfers between devices  198 us
    all_gather x1, waiting for transfers between devices, per_device(): group_set = lax.all_gather(holdings, 'ray', axis=0, tiled=True)  77.1 us
    all_to_all x1, blocking collectives, per_device(): lax.all_to_all(outgoing, 'group', split_axis=0, concat_axis=0, tiled=True)  19.3 us
    all_to_all x1, blocking collectives, per_device(): lax.all_to_all(requests, 'group', split_axis=0, concat_axis=0, tiled=True)  16.4 us
    dot_general x1, local copies, waits for them, and re-layouts, per_device(): jnp.einsum('tiv,tic->tvc', weights_tiles, grads_tiles, preferred_element_...  11.8 us
    scatter-add x1, other arithmetic, per_device(): jax.ops.segment_sum(outer.reshape(tiles_dev, row_width), slots, num_segme...  10.6 us
    all_to_all x1, blocking collectives, per_device(): lax.all_to_all(picked, 'group', split_axis=0, concat_axis=0, tiled=True)  10.4 us
    select_n x1, local copies, waits for them, and re-layouts, per_device(): jnp.take(group_set, slots, axis=0).reshape(tiles_dev, voxels, channels)  10.1 us
  transfers between devices with their start and end apart: 2, of which 2 were waited for; matrix products, arithmetic and copies ran while one was open for 1% of the time, Pallas kernels for 0%

commit v1 on v0

--- a/solution.py
+++ b/solution.py
@@ -74,7 +74,9 @@
     )
     fetched = lax.all_to_all(picked, "group", split_axis=0, concat_axis=0, tiled=True)
     holdings = fetched[owner_group, entry_rank]
-    group_set = lax.all_gather(holdings, "ray", axis=0, tiled=True)
+    group_set = jnp.concatenate(
+        lax.all_to_all(jnp.stack([holdings] * lax.axis_size("ray")), "ray", 0, 0), axis=0
+    )
     weights_tiles = interp.reshape(tiles_dev, samples, voxels)
     slots = tile_slot.reshape(-1)
     tiles = jnp.take(group_set, slots, axis=0).reshape(tiles_dev, voxels, channels)

time: 439 us -> 393 us (0.90)
  waiting for transfers between devices: 275 us -> 215 us
  starting transfers between devices: 0.04 us -> 13.2 us
    all_gather x1 -> x0, waiting for transfers between devices: 77.1 us -> none  [per_device(): group_set = lax.all_gather(holdings, 'ray', axis=0, tiled=True)]
    all_to_all x0 -> x1, waiting for transfers between devices: none -> 23.1 us  [per_device(): lax.all_to_all(jnp.stack([holdings] * lax.axis_size('ray')), 'ray', 0, 0)]
    all_to_all x0 -> x1, starting transfers between devices: none -> 13.1 us  [per_device(): lax.all_to_all(jnp.stack([holdings] * lax.axis_size('ray')), 'ray', 0, 0)]
    unnamed x3 -> x2, waiting for transfers between devices: 198 us -> 192 us
where the time goes in v1:
time: 393 us; the launch traced here: 392 us
  waiting for transfers between devices  215 us (55%)
  local copies, waits for them, and re-layouts  53.9 us (14%)
  blocking collectives  46.1 us (12%)
  other arithmetic  29.4 us (7%)
  matrix products  19.7 us (5%)
  between operations  14.3 us (4%)
  starting transfers between devices  13.2 us (3%)
    unnamed x2, waiting for transfers between devices  192 us
    all_to_all x1, waiting for transfers between devices, per_device(): lax.all_to_all(jnp.stack([holdings] * lax.axis_size('ray')), 'ray', 0, 0)  23.1 us
    all_to_all x1, blocking collectives, per_device(): lax.all_to_all(outgoing, 'group', split_axis=0, concat_axis=0, tiled=True)  19.3 us
    all_to_all x1, blocking collectives, per_device(): lax.all_to_all(requests, 'group', split_axis=0, concat_axis=0, tiled=True)  16.4 us
    all_to_all x1, starting transfers between devices, per_device(): lax.all_to_all(jnp.stack([holdings] * lax.axis_size('ray')), 'ray', 0, 0)  13.1 us
    dot_general x1, local copies, waits for them, and re-layouts, per_device(): jnp.einsum('tiv,tic->tvc', weights_tiles, grads_tiles, preferred_element_...  11.8 us
    scatter-add x1, other arithmetic, per_device(): jax.ops.segment_sum(outer.reshape(tiles_dev, row_width), slots, num_segme...  10.6 us
    all_to_all x1, blocking collectives, per_device(): lax.all_to_all(picked, 'group', split_axis=0, concat_axis=0, tiled=True)  10.4 us
  transfers between devices with their start and end apart: 2, of which 2 were waited for; matrix products, arithmetic and copies ran while one was open for 1% of the time, Pallas kernels for 0%

profile of v1, /device:TPU:31, one launch (start us, length us, event | category | flops | bytes accessed | tf_op | source)
XLA Modules:
  0.0 391.7 jit_solution(10210058238951387267)
XLA Ops:
  9.5 16.4 %all_to_all.30 = s32[8,1,2]{2,1,0:T(1,128)S(1)} all-to-all(s32[8,1,2]{2,1,0:T(1,128)S(1)} %copy.55), channel_id=1, replica_groups=mesh['group'=8,'ray'=64] {'group'}, dimensions={0} | all-to-all | bytes 128 | tf_op jit(solution)/shard_map/all_to_all | solution.py:67
  29.0 10.4 %all_to_all.31 = bf16[8,2,4096]{2,1,0:T(2,128)(2,1)S(1)} all-to-all(bf16[8,2,4096]{2,1,0:T(2,128)(2,1)S(1)} %broadcast_select_fusion.2), channel_id=1, replica_groups=mesh['group'=8,'ray'=64] {'group'}, dimensions={0} | all-to-all | bytes 262144 | tf_op jit(solution)/shard_map/all_to_all | solution.py:75
  40.1 2.0 stack.2
  42.1 13.1 %all-to-all-start.2 = ((bf16[64,2,4096]{2,1,0:T(2,128)(2,1)}), bf16[64,2,4096]{2,1,0:T(2,128)(2,1)S(1)}, u32[]{:S(2)}, u32[]{:S(2)}) async-start(bf16[64,2,4096]{2,1,0:T(2,128)(2,1)} %stack.2), calls=%async_computation.2 | async-start | bytes 2097152 | tf_op jit(solution)/shard_map/all_to_all | solution.py:78
  57.9 23.1 %all-to-all-done.2 = bf16[64,2,4096]{2,1,0:T(2,128)(2,1)S(1)} async-done(((bf16[64,2,4096]{2,1,0:T(2,128)(2,1)}), bf16[64,2,4096]{2,1,0:T(2,128)(2,1)S(1)}, u32[]{:S(2)}, u32[]{:S(2)}) %all-to-all-start.2) | async-done | bytes 1048608 | tf_op jit(solution)/shard_map/all_to_all | solution.py:78
  81.4 3.9 gather_fusion.2
  85.3 3.3 copy.61
  88.6 2.0 broadcast_select_fusion
  90.6 10.1 %copy.63 = bf16[320,64,64]{2,1,0:T(8,128)(2,1)} copy(bf16[320,64,64]{0,2,1:T(8,128)(2,1)} %broadcast_select_fusion) | data formatting | bytes 5242880 | tf_op jit(solution)/shard_map/jit(_take)/select_n | solution.py:82
  100.7 4.3 %fusion.8 = f32[2560,256]{1,0:T(8,128)S(1)} fusion(bf16[64,256]{1,0:T(8,128)(2,1)} %param.15, bf16[320,64,64]{2,1,0:T(8,128)(2,1)} %copy.63, bf16[320,8,64]{2,1,0:T(8,128)(2,1)S(1)} %copy-done.1), kind=kOutput, calls=%fused_computation.25 | convolution fusion | flops 105021440 | bytes 5603328 | tf_op jit(solution)/shard_map/dot_general | solution.py:23
  105.1 1.7 fusion.4
  109.7 1.6 reshape.285
  112.7 1.6 reduce_window_sum.22
  116.1 1.6 fusion.12
  119.7 1.6 reduce_window_sum.23
  123.8 1.6 convert_element_type.36
  125.4 4.0 %fusion = bf16[2560,256]{1,0:T(8,128)(2,1)} fusion(bf16[2560,4]{0,1:T(4,128)(2,1)} %convert_element_type.36, bf16[256,4]{0,1:T(4,128)(2,1)S(1)} %copy-done.7, f32[2560,256]{1,0:T(8,128)} %copy-done.8), kind=kOutput, calls=%fused_computation.9 | convolution fusion | flops 11141120 | bytes 3954688 | tf_op jit(solution)/shard_map/dot_general | solution.py:31
  129.3 3.3 convolution_convert_fusion
  134.0 4.9 %convolution_bitcast_fusion = f32[320,64,64]{1,2,0:T(8,128)} fusion(bf16[320,8,64]{2,1,0:T(8,128)(2,1)S(1)} %copy-done.1, bf16[2560,64]{1,0:T(8,128)(2,1)S(1)} %copy.66), kind=kOutput, calls=%fused_computation.11 | convolution fusion | flops 20971520 | bytes 5898240 | tf_op jit(solution)/shard_map/tiv,tic->tvc/dot_general | solution.py:87
  138.9 11.8 %copy.67 = f32[320,64,64]{0,2,1:T(8,128)} copy(f32[320,64,64]{1,2,0:T(8,128)} %convolution_bitcast_fusion) | data formatting | bytes 10485760 | tf_op jit(solution)/shard_map/tiv,tic->tvc/dot_general | solution.py:87
  150.7 6.2 %copy.68 = f32[320,4096]{1,0:T(8,128)} copy(f32[320,4096]{0,1:T(8,128)} %bitcast.96) | data formatting | bytes 10485760 | tf_op jit(solution)/shard_map/reshape | solution.py:91
  156.9 10.6 %scatter_custom_fusion.1 = f32[128,4096]{1,0:T(8,128)} fusion(s32[320]{0:T(512)S(1)} %reshape.319, f32[320,4096]{1,0:T(8,128)} %copy.68, f32[]{:T(128)} %constant.85.clone.1), kind=kCustom, calls=%fused_computation.23 | custom fusion | flops 1310720 | bytes 2097664 | tf_op jit(solution)/shard_map/scatter-add | solution.py:90
  169.4 192.1 %all-reduce.5.cloned.1.call-done = f32[128,4096]{1,0:T(8,128)} async-done(((f32[128,4096]{1,0:T(8,128)}), f32[128,4096]{1,0:T(8,128)}) %all-reduce.5.cloned.1.call-update) | async-done | bytes 2097168
  363.3 19.3 %all_to_all.32 = f32[8,2,4096]{2,1,0:T(2,128)S(1)} all-to-all(f32[8,2,4096]{2,1,0:T(2,128)S(1)} %scatter_fusion.1), channel_id=1, replica_groups=mesh['group'=8,'ray'=64] {'group'}, dimensions={0} | all-to-all | bytes 524288 | tf_op jit(solution)/shard_map/all_to_all | solution.py:99
  (67 shorter events, 26.8 us)
Async XLA Ops:
  6.5 21.2 %copy-start = (bf16[32,4096]{1,0:T(8,128)(2,1)S(1)}, bf16[32,4096]{1,0:T(8,128)(2,1)}, u32[]{:S(2)}) copy-start(bf16[32,4096]{1,0:T(8,128)(2,1)} %param.9) | copy-start | bytes 786436
  27.7 27.5 %copy-start.5 = (s32[64,5]{0,1:T(8,128)S(1)}, s32[64,5]{0,1:T(8,128)}, u32[]{:S(2)}) copy-start(s32[64,5]{0,1:T(8,128)} %param.12) | copy-start | bytes 3844
  27.7 27.9 %copy-start.2 = (bf16[64,5,512]{2,0,1:T(8,128)(2,1)S(1)}, bf16[64,5,512]{2,0,1:T(8,128)(2,1)}, u32[]{:S(2)}) copy-start(bf16[64,5,512]{2,0,1:T(8,128)(2,1)} %param.11) | copy-start | bytes 983044
  40.0 17.1 %copy-start.4 = (f32[64,40]{0,1:T(8,128)S(1)}, f32[64,40]{0,1:T(8,128)}, u32[]{:S(2)}) copy-start(f32[64,40]{0,1:T(8,128)} %param.13) | copy-start | bytes 30724
  42.1 39.0 %all-to-all-start.2 = ((bf16[64,2,4096]{2,1,0:T(2,128)(2,1)}), bf16[64,2,4096]{2,1,0:T(2,128)(2,1)S(1)}, u32[]{:S(2)}, u32[]{:S(2)}) async-start(bf16[64,2,4096]{2,1,0:T(2,128)(2,1)} %stack.2), calls=%async_computation.2 | async-start | bytes 2097152 | tf_op jit(solution)/shard_map/all_to_all | solution.py:78
  55.2 306.4 %all-reduce.5.cloned.1.call-start = ((), (), s32[]{:S(2)}) async-start(), calls=%async_computation.4 | async-start | bytes 4194304
  90.6 10.1 %copy-start.1 = (bf16[320,8,64]{2,1,0:T(8,128)(2,1)S(1)}, bf16[320,8,64]{2,1,0:T(8,128)(2,1)}, u32[]{:S(2)}) copy-start(bf16[320,8,64]{2,1,0:T(8,128)(2,1)} %reshape.283) | copy-start | bytes 983044
  105.0 3.3 copy-start.7
  106.8 1.5 copy-start.8
  108.3 7.8 %copy-start.6 = (f32[3,64]{1,0:T(4,128)S(1)}, f32[3,64]{1,0:T(4,128)}, u32[]{:S(2)}) copy-start(f32[3,64]{1,0:T(4,128)} %param.14) | copy-start | bytes 2308
  117.7 0.6 copy-start.3
Sparse Core Ops, SparseCore 0:
  167.6 193.8 all-reduce.4
